TPU v7x, 32 devices: a whole 2x2x4 slice. The times are simulated.
32 devices in a mesh: fsdp: 8 (over z, x), seq: 4 (over y, core).
Axes of the slice: x: 2, y: 2, z: 4, core: 2. Of those that a mesh axis runs over, the one named last changes fastest.
Arguments:
- context: bfloat16 [16, 512, 2560], P('fsdp', 'seq'), may hold values from -6 to 6
- residual: bfloat16 [16, 512, 2560], P('fsdp', 'seq'), may hold values from -6 to 6
- target_rows: bfloat16 [16, 512, 2560], P('fsdp', 'seq'), may hold values from -0.00390625 to 0.00390625
- log_norm: float32 [16, 512], P('fsdp', 'seq'), may hold values from -0.15 to 0.15
- norm_gain: float32 [2560], replicated, may hold values from 0.1 to 1.9
- out_proj: bfloat16 [2560, 2560], P('fsdp'), may hold values from -0.125 to 0.125
- old_logprob: float32 [16, 512], P('fsdp', 'seq'), may hold values from -0.15 to 0.15
- lengths: int32 [16, 4], P('fsdp', 'seq'), may hold values from 112 to 128
- rewards: float32 [16, 4], P('fsdp', 'seq'), may hold values from -5 to 5
- prompt_ids: int32 [16, 4], P('fsdp', 'seq'), may hold values from 0 to 3, as said below
- placement: int32 [16, 4], P('fsdp', 'seq'), may hold values from 0 to 15, as said below
Outputs:
- grad_context: bfloat16 [16, 512, 2560], P('fsdp', 'seq')
- grad_weight: float32 [2560, 2560], P('fsdp')
- loss: float32 [], replicated
Inputs may be any that keep to these rules, and one draw needn't show every extreme that they name: `prompt_ids`: every prompt id names exactly 16 rows. Sampler row (a, s) goes to learner row (placement[a, s], s) and keeps a mod 2; the 2 rows of one device go to 2 different fsdp indices; every learner row receives exactly one row; in every column one of the 2 rows of each device goes 8 / 2 fsdp indices onward and another goes 1 index onward, counted round.
All inputs are finite; a program needn't handle non-finite values.
Results may differ from a plain program's by a relative error of at most 0.014.
Values may be sent and summed in bfloat16 or wider, within the bound.
A program may use at most 128 MiB of HBM per device.

v0:
```python
import math

import jax
import jax.numpy as jnp
from jax import lax
from jax.sharding import PartitionSpec as P

DW = 2560
AW = 2560
GS = 16


def body(
    context,
    residual,
    target_rows,
    log_norm,
    norm_gain,
    out_proj,
    old_logprob,
    lengths,
    rewards,
    prompt_ids,
    placement,
):
    nrows = context.shape[0]
    lmax = context.shape[1]
    fsdp_ways = lax.axis_size("fsdp")
    seq_ways = lax.axis_size("seq")
    prompts = nrows * fsdp_ways * seq_ways // GS
    all_tokens = nrows * lmax * fsdp_ways * seq_ways
    reward_flat = rewards.reshape(-1)
    prompt_flat = prompt_ids.reshape(-1)
    length_flat = lengths.reshape(-1)
    dest_flat = placement.reshape(-1)
    prompt_range = jnp.arange(prompts, dtype=jnp.int32)
    local_hot = (prompt_flat[:, None] == prompt_range[None, :]).astype(jnp.float32)
    group_sum, group_sq, count = lax.psum(
        (
            jnp.sum(local_hot * reward_flat[:, None], axis=0),
            jnp.sum(local_hot * (reward_flat * reward_flat)[:, None], axis=0),
            jnp.sum(length_flat.astype(jnp.float32)),
        ),
        ("fsdp", "seq"),
    )
    group_mean = group_sum / GS
    group_var = group_sq / GS - group_mean * group_mean
    row_mean = jnp.sum(local_hot * group_mean[None, :], axis=1)
    row_var = jnp.sum(local_hot * group_var[None, :], axis=1)
    advantage = (reward_flat - row_mean) / jnp.sqrt(row_var + 0.25)
    slots = jnp.arange(nrows, dtype=jnp.int32)
    every_old, every_adv, every_len, every_dest = (
        lax.all_gather(old_logprob, "fsdp", axis=0, tiled=True),
        lax.all_gather(advantage, "fsdp", axis=0, tiled=True),
        lax.all_gather(length_flat, "fsdp", axis=0, tiled=True),
        lax.all_gather(dest_flat, "fsdp", axis=0, tiled=True),
    )
    wanted = lax.axis_index("fsdp") * nrows + slots
    chosen = every_dest[None, :] == wanted[:, None]
    learn_old = jnp.sum(jnp.where(chosen[:, :, None], every_old[None, :, :], 0.0), axis=1)
    learn_adv = jnp.sum(jnp.where(chosen, every_adv[None, :], 0.0), axis=1)
    learn_len = jnp.sum(jnp.where(chosen, every_len[None, :], 0), axis=1)
    offsets = jnp.arange(lmax, dtype=jnp.int32)
    valid = (offsets[None, :] < learn_len[:, None]).astype(jnp.float32).reshape(-1)
    token_adv = jnp.broadcast_to(learn_adv[:, None], (nrows, lmax)).reshape(-1)
    tokens = nrows * lmax
    context_flat = context.reshape(tokens, AW)
    whole = lax.all_gather(out_proj, "fsdp", axis=0, tiled=True)
    hidden = residual.reshape(tokens, DW).astype(jnp.float32) + jnp.dot(
        context_flat, whole, preferred_element_type=jnp.float32
    )
    rinv = lax.rsqrt(jnp.mean(hidden * hidden, axis=1) + 1e-06)
    vecs = norm_gain[None, :] * target_rows.reshape(tokens, DW).astype(jnp.float32)
    hv_sum = jnp.sum(hidden * vecs, axis=1)
    score = hv_sum * rinv
    ratio = jnp.exp(score - log_norm.reshape(-1) - learn_old.reshape(-1))
    plain = ratio * token_adv
    clipped = jnp.clip(ratio, 0.8, 1.2) * token_adv
    objective = jnp.minimum(plain, clipped)
    loss_local = jnp.sum(valid * -objective)
    dscore = -valid * jnp.where(plain <= clipped, plain, 0.0) / count
    dhid = (dscore * rinv)[:, None] * (vecs - hidden * (rinv * rinv * hv_sum / DW)[:, None])
    grad_hidden = (dhid * (32.0 * all_tokens * math.sqrt(DW))).astype(jnp.bfloat16)
    grad_context = lax.dot_general(
        grad_hidden, whole, (((1,), (1,)), ((), ())), preferred_element_type=jnp.float32
    ).astype(jnp.bfloat16)
    piece = lax.psum_scatter(
        lax.dot_general(
            context_flat, grad_hidden, (((0,), (0,)), ((), ())), preferred_element_type=jnp.float32
        ).astype(jnp.bfloat16),
        "fsdp",
        scatter_dimension=0,
        tiled=True,
    )
    grad_weight = lax.psum(piece, "seq").astype(jnp.float32) * (1.0 / math.sqrt(all_tokens))
    loss = lax.psum(loss_local, ("fsdp", "seq")) / count
    return (grad_context.reshape(nrows, lmax, AW), grad_weight, loss)


def solution(mesh):
    return jax.shard_map(
        body,
        mesh=mesh,
        in_specs=(
            P("fsdp", "seq", None),
            P("fsdp", "seq", None),
            P("fsdp", "seq", None),
            P("fsdp", "seq"),
            P(),
            P("fsdp", None),
            P("fsdp", "seq"),
            P("fsdp", "seq"),
            P("fsdp", "seq"),
            P("fsdp", "seq"),
            P("fsdp", "seq"),
        ),
        out_specs=(P("fsdp", "seq", None), P("fsdp", None), P()),
        check_vma=False,
    )
```

profile of v0, /device:TPU:1, one launch (start us, length us, event | category | flops | bytes accessed | tf_op | source)
XLA Modules:
  0.0 558.5 jit_solution(6872598172934750625)
XLA Ops:
  8.6 0.8 select_reduce_fusion.6
  9.4 45.7 %all-reduce.5 = (f32[4]{0:T(128)S(1)}, f32[4]{0:T(128)S(1)}) all-reduce(f32[4]{0:T(128)S(1)} %get-tuple-element.16, f32[4]{0:T(128)S(1)} %get-tuple-element.17), channel_id=1, replica_groups=mesh['fsdp'=8,'seq'=4] {'fsdp','seq'}, use_global_device_ids=true, to_apply=%region_5.0 | all-reduce | flops 8 | bytes 64 | tf_op jit(solution)/shard_map/psum | solution.py:38
  55.1 1.2 dynamic-slice
  57.0 0.9 select_reduce_fusion.5
  57.8 0.8 bitcast_dynamic-update-slice_fusion.1
  58.6 0.7 multiply_dynamic-update-slice_fusion
  59.3 0.7 bitcast_dynamic-update-slice_fusion
  60.1 14.7 %all-reduce.2 = f32[16]{0:T(128)S(1)} all-reduce(f32[16]{0:T(128)S(1)} %multiply_dynamic-update-slice_fusion), channel_id=1, replica_groups=mesh['fsdp'=8,'seq'=4] {'fsdp'}, use_global_device_ids=true, to_apply=%add.2 | all-reduce | flops 16 | bytes 128
  74.8 6.9 %all-reduce.3 = (s32[16]{0:T(128)S(1)}, s32[16]{0:T(128)S(1)}) all-reduce(s32[16]{0:T(128)S(1)} %bitcast_dynamic-update-slice_fusion.1, s32[16]{0:T(128)S(1)} %bitcast_dynamic-update-slice_fusion), channel_id=2, replica_groups=mesh['fsdp'=8,'seq'=4] {'fsdp'}, use_global_device_ids=true, to_apply=%add | all-reduce | flops 32 | bytes 256
  81.7 16.4 %all-gather.2 = f32[8,2,128]{2,1,0:T(2,128)S(1)} all-gather(f32[1,2,128]{2,1,0:T(2,128)} %bitcast.68), channel_id=1, replica_groups=mesh['fsdp'=8,'seq'=4] {'fsdp'}, dimensions={0}, use_global_device_ids=true | all-gather | bytes 9216 | tf_op jit(solution)/shard_map/all_gather | solution.py:53
  98.0 1.3 convert_reduce_fusion
  99.7 96.3 %all-gather.5.cloned.1.call-done = bf16[2560,2560]{1,0:T(8,128)(2,1)} async-done(((bf16[320,2560]{1,0:T(8,128)(2,1)}), bf16[2560,2560]{1,0:T(8,128)(2,1)}) %all-gather.5.cloned.1.call-update) | async-done | bytes 13107216 | tf_op jit(solution)/shard_map/all_gather | solution.py:68
  196.0 10.4 %multiply_reduce_fusion = (f32[256]{0:T(256)S(1)}, f32[256]{0:T(256)S(1)}, f32[256,2560]{1,0:T(8,128)}) fusion(bf16[2,128,2560]{2,1,0:T(8,128)(2,1)} %param.13, f32[2560]{0:T(1024)} %param.15, bf16[256,2560]{1,0:T(8,128)(2,1)S(1)} %bitcast.62, bf16[2560,2560]{1,0:T(8,128)(2,1)} %all-gather.5.cloned.1.call-done, bf16[256,2560]{1,0:T(8,128)(2,1)} %bitcast.69), kind=kOutput, calls=%fused_computation.12 | convolution fusion | flops 3360685568 | bytes 19673088 | tf_op jit(solution)/shard_map/dot_general | solution.py:69
  207.1 38.4 %all-reduce.4 = (f32[]{:T(128)}, f32[]{:T(128)}) all-reduce(f32[]{:T(128)} %convert_reduce_fusion, f32[]{:T(128)} %select_reduce_fusion.1), channel_id=1, replica_groups=mesh['fsdp'=8,'seq'=4] {'fsdp','seq'}, use_global_device_ids=true, to_apply=%region_12.13 | all-reduce | flops 2 | bytes 16 | tf_op jit(solution)/shard_map/psum | solution.py:38
  245.5 0.7 divide_multiply_fusion
  246.2 2.7 fusion.6
  249.0 6.8 %fusion = bf16[2560,2560]{0,1:T(8,128)(2,1)} fusion(bf16[256,2560]{1,0:T(8,128)(2,1)S(1)} %fusion.6, bf16[256,2560]{1,0:T(8,128)(2,1)S(1)} %bitcast.63), kind=kOutput, calls=%fused_computation.1 | convolution fusion | flops 3361996800 | bytes 15728640 | tf_op jit(solution)/shard_map/dot_general | solution.py:88
  255.7 17.6 %copy.17 = bf16[2560,2560]{1,0:T(8,128)(2,1)} copy(bf16[2560,2560]{0,1:T(8,128)(2,1)} %fusion) | data formatting | bytes 26214400
  274.8 214.9 %reduce-scatter.4.cloned.1.call-done = bf16[320,2560]{1,0:T(8,128)(2,1)} async-done(((bf16[2560,2560]{1,0:T(8,128)(2,1)}), bf16[320,2560]{1,0:T(8,128)(2,1)}) %reduce-scatter.4.cloned.1.call-update) | async-done | bytes 1638416
  489.6 3.8 copy.18
  493.5 9.4 %convolution_convert_fusion.1 = bf16[256,2560]{1,0:T(8,128)(2,1)} fusion(bf16[256,2560]{1,0:T(8,128)(2,1)S(1)} %fusion.6, bf16[2560,2560]{1,0:T(8,128)(2,1)} %all-gather.5.cloned.1.call-done), kind=kOutput, calls=%fused_computation.4 | convolution fusion | flops 3356098560 | bytes 15728640 | tf_op jit(solution)/shard_map/dot_general | solution.py:84
  502.8 39.0 %all-reduce.8.cloned.1.call-done = bf16[320,2560]{0,1:T(8,128)(2,1)} async-done(((bf16[320,2560]{0,1:T(8,128)(2,1)}), bf16[320,2560]{0,1:T(8,128)(2,1)}) %all-reduce.8.cloned.1.call-update) | async-done | bytes 1638416 | tf_op jit(solution)/shard_map/psum | solution.py:95
  541.9 3.8 convert_multiply_fusion
  545.6 5.2 copy.16
  (22 shorter events, 2.6 us)
Async XLA Ops:
  7.2 188.9 %copy-start = (bf16[2,128,2560]{2,1,0:T(8,128)(2,1)S(1)}, bf16[2,128,2560]{2,1,0:T(8,128)(2,1)}, u32[]{:S(2)}) copy-start(bf16[2,128,2560]{2,1,0:T(8,128)(2,1)} %param.11) | copy-start | bytes 3932164
  7.2 188.8 %all-gather.5.cloned.1.call-start = ((), (), s32[]{:S(2)}) async-start(), calls=%async_computation.1 | async-start | bytes 14745600 | tf_op jit(solution)/shard_map/all_gather | solution.py:68
  7.9 481.7 %reduce-scatter.4.cloned.1.call-start = ((), (), s32[]{:S(2)}) async-start(), calls=%async_computation.3 | async-start | bytes 14745600
  196.0 10.4 %copy-start.2 = (f32[2,128]{1,0:T(2,128)S(1)}, f32[2,128]{1,0:T(2,128)}, u32[]{:S(2)}) copy-start(f32[2,128]{1,0:T(2,128)} %param.14) | copy-start | bytes 3076
  196.0 50.2 %copy-start.1 = (f32[2560]{0:T(1024)S(1)}, f32[2560]{0:T(1024)}, u32[]{:S(2)}) copy-start(f32[2560]{0:T(1024)} %param.15) | copy-start | bytes 30724
  273.4 268.5 %all-reduce.8.cloned.1.call-start = ((), (), s32[]{:S(2)}) async-start(), calls=%async_computation.2 | async-start | bytes 3932160 | tf_op jit(solution)/shard_map/psum | solution.py:95
Sparse Core Ops, SparseCore 0:
  10.2 185.7 all-gather.4
  273.5 216.0 reduce-scatter.3
  493.6 48.2 all-reduce.7
where the time goes:
time: 560 us; the launch traced here: 559 us
  waiting for transfers between devices  351 us (63%)
  blocking collectives  122 us (22%)
  local copies, waits for them, and re-layouts  29.4 us (5%)
  matrix products  26.5 us (5%)
  between operations  16.9 us (3%)
  other arithmetic  12.6 us (2%)
    unnamed x4, waiting for transfers between devices  216 us
    all_gather x1, waiting for transfers between devices, body(): whole = lax.all_gather(out_proj, 'fsdp', axis=0, tiled=True)  96.3 us
    psum x2, blocking collectives, body(): lax.psum((jnp.sum(local_hot * reward_flat[:, None], axis=0), jnp.sum(loca...  84.1 us
    psum x1, waiting for transfers between devices, body(): lax.psum(piece, 'seq').astype(jnp.float32) * (1.0 / math.sqrt(all_tokens))  39 us
    unnamed x15, local copies, waits for them, and re-layouts  29.4 us
    unnamed x2, blocking collectives  21.6 us
    all_gather x1, blocking collectives, body(): lax.all_gather(old_logprob, 'fsdp', axis=0, tiled=True)  16.4 us
  transfers between devices with their start and end apart: 3, of which 3 were waited for; matrix products, arithmetic and copies ran while one was open for 3% of the time, Pallas kernels for 0%

commit v1 on v0

v1 whole, which is shorter than its diff:
```python
import functools
import math

import jax
import jax.numpy as jnp
from jax import lax
from jax.experimental import pallas as pl
from jax.experimental.pallas import tpu as pltpu
from jax.sharding import PartitionSpec as P

GS = 16
FO = 4
Q = 4
MESH = pl.DeviceIdType.MESH
F32 = jnp.float32
BF16 = jnp.bfloat16


def kernel(
    dims,
    ctx,
    res,
    tgt,
    lognorm,
    gain,
    wown,
    packet,
    gctx,
    gw,
    loss_out,
    w,
    ctxt,
    hid,
    ghs,
    ghr,
    dws,
    irecv,
    part,
    obuf,
    orecv,
    fsend,
    frecv,
    pk,
    ls,
    ag_o,
    ag_i,
    ag_c,
    cx,
    gx,
    rs_i,
    rs_o,
    fin,
    pk1,
    pk2,
    pk3,
    ls1,
    ls2,
    ls3,
):
    fsdp_ways, seq_ways, nrows, lmax, dw, aw = dims
    fi = fsdp_ways // FO
    so_ways = seq_ways // Q
    tokens = nrows * lmax
    blk = aw // fsdp_ways
    cq = dw // Q
    prompts = nrows * fsdp_ways * seq_ways // GS
    prows = max(8, prompts)
    all_tokens = tokens * fsdp_ways * seq_ways
    f = lax.axis_index("fsdp")
    s = lax.axis_index("seq")
    o = f // fi
    i = lax.rem(f, fi)
    so = s // Q
    q = lax.rem(s, Q)
    c = lax.rem(q, 2)

    def outer_dev(k, m=0):
        return (lax.rem(o + k, FO) * fi + i, lax.rem(so + m, so_ways) * Q + q)

    def inner_dev(j):
        return (o * fi + lax.rem(i + j, fi), s)

    def group_dev(k):
        return (f, so * Q + lax.rem(q + k, Q))

    core_dev = (f, so * Q + q + 1 - 2 * c)
    outer = [(m, k) for k in range(FO) for m in range(so_ways) if (m, k) != (0, 0)]
    barrier = pltpu.get_barrier_semaphore()
    peers = [outer_dev(k, m) for m, k in outer]
    peers += [inner_dev(j) for j in range(1, fi)]
    peers += [group_dev(k) for k in range(1, Q)]
    for peer in peers:
        pl.semaphore_signal(barrier, inc=1, device_id=peer, device_id_type=MESH)
    pl.semaphore_wait(barrier, len(peers))

    sent = []

    def send(src, dst, sems, index, dev):
        copy = pltpu.make_async_remote_copy(
            src_ref=src,
            dst_ref=dst,
            send_sem=sems.at[(0,) + index],
            recv_sem=sems.at[(1,) + index],
            device_id=dev,
            device_id_type=MESH,
        )
        copy.start()
        sent.append(copy)

    def arrive(dst, sems, index, dev):
        pltpu.make_async_remote_copy(
            src_ref=dst,
            dst_ref=dst,
            send_sem=sems.at[(0,) + index],
            recv_sem=sems.at[(1,) + index],
            device_id=dev,
            device_id_type=MESH,
        ).wait_recv()

    def rows_of(owner):
        return pl.ds(pl.multiple_of(owner * blk, blk), blk)

    def half(owner, side):
        return w.at[pl.ds(2 * side, 2), rows_of(owner), :]

    pk[o, so, i, q] = packet[...]
    for k in range(1, Q):
        mine = pk.at[o, so, i, q]
        send(mine, mine, pk1, (k,), group_dev(k))

    for part_q in range(Q):
        w[part_q, rows_of(f), :] = wown[:, part_q * cq : (part_q + 1) * cq]
    for k in (2, 1, 3):
        send(half(f, c), half(f, c), ag_o, (k,), outer_dev(k))
    for j in range(1, fi):
        send(half(f, c), half(f, c), ag_i, (0, j), inner_dev(j))

    @pl.loop(0, aw // 256)
    def _(t):
        span = pl.ds(pl.multiple_of(t * 256, 256), 256)
        ctxt[q, span, :] = ctx[:, span].T

    for k in range(1, Q):
        send(ctxt.at[q], ctxt.at[q], cx, (k,), group_dev(k))

    for k in range(1, Q):
        there = pk.at[o, so, i, lax.rem(q + Q - k, Q)]
        arrive(there, pk1, (k,), group_dev(k))
    for j in range(1, fi):
        mine = pk.at[o, so, i]
        send(mine, mine, pk2, (j,), inner_dev(j))
    for j in range(1, fi):
        there = pk.at[o, so, lax.rem(i + fi - j, fi)]
        arrive(there, pk2, (j,), inner_dev(j))
    for m, k in outer:
        mine = pk.at[o, so]
        send(mine, mine, pk3, (m, k), outer_dev(k, m))
    for m, k in outer:
        there = pk.at[lax.rem(o + FO - k, FO), lax.rem(so + so_ways - m, so_ways)]
        arrive(there, pk3, (m, k), outer_dev(k, m))

    prompt_row = lax.broadcasted_iota(jnp.int32, (prows, 128), 0).astype(F32)
    zero_p = jnp.zeros((prows, 128), F32)
    zero_r = jnp.zeros((1, 128), F32)

    def over_devices(fa, carry):
        for sa in range(seq_ways):
            at = (fa // fi, sa // Q, lax.rem(fa, fi), sa % Q)
            for r in range(nrows):
                gsum, gsq, count = carry
                reward = pk[at + (pl.ds(nrows + r, 1), slice(None))]
                prompt = pk[at + (pl.ds(2 * nrows + r, 1), slice(None))]
                length = pk[at + (pl.ds(3 * nrows + r, 1), slice(None))]
                hot = prompt == prompt_row
                gsum = gsum + jnp.where(hot, reward, 0.0)
                gsq = gsq + jnp.where(hot, reward * reward, 0.0)
                carry = (gsum, gsq, count + length)
        return carry

    gsum, gsq, count = lax.fori_loop(0, fsdp_ways, over_devices, (zero_p, zero_p, zero_r))
    gmean = gsum / GS
    gvar = gsq / GS - gmean * gmean

    def over_column(fa, carry):
        at = (fa // fi, so, lax.rem(fa, fi), q)
        for r in range(nrows):
            old = pk[at + (pl.ds(r, 1), slice(None))]
            reward = pk[at + (pl.ds(nrows + r, 1), slice(None))]
            prompt = pk[at + (pl.ds(2 * nrows + r, 1), slice(None))]
            length = pk[at + (pl.ds(3 * nrows + r, 1), slice(None))]
            dest = pk[at + (pl.ds(4 * nrows + r, 1), slice(None))]
            hot = prompt == prompt_row
            mean = jnp.sum(jnp.where(hot, gmean, 0.0), axis=0, keepdims=True)
            var = jnp.sum(jnp.where(hot, gvar, 0.0), axis=0, keepdims=True)
            adv = (reward - mean) / jnp.sqrt(var + 0.25)
            fresh = []
            for j in range(nrows):
                chosen = dest == (f * nrows + j).astype(F32)
                l_old, l_adv, l_len = carry[3 * j : 3 * j + 3]
                fresh += [
                    l_old + jnp.where(chosen, old, 0.0),
                    l_adv + jnp.where(chosen, adv, 0.0),
                    l_len + jnp.where(chosen, length, 0.0),
                ]
            carry = tuple(fresh)
        return carry

    learned = lax.fori_loop(0, fsdp_ways, over_column, (zero_r,) * (3 * nrows))
    eye_r = lax.broadcasted_iota(jnp.int32, (lmax, lmax), 0)
    eye_c = lax.broadcasted_iota(jnp.int32, (lmax, lmax), 1)
    offset = lax.broadcasted_iota(jnp.int32, (lmax, 1), 0).astype(F32)

    def upright(row):
        spread = jnp.broadcast_to(row, (lmax, lmax))
        return jnp.sum(jnp.where(eye_r == eye_c, spread, 0.0), axis=1, keepdims=True)

    base, token_adv, valid = [], [], []
    for j in range(nrows):
        l_old, l_adv, l_len = learned[3 * j : 3 * j + 3]
        base.append(upright(lognorm[pl.ds(j, 1), :]) + upright(l_old))
        token_adv.append(jnp.broadcast_to(l_adv[:, 0:1], (lmax, 1)))
        valid.append((offset < l_len[:, 0:1]).astype(F32))
    base = jnp.concatenate(base, axis=0)
    token_adv = jnp.concatenate(token_adv, axis=0)
    valid = jnp.concatenate(valid, axis=0)
    count1 = count[:, 0:1]

    def onward(owner):
        send(half(owner, c), half(owner, c), ag_c, (owner,), core_dev)

    for j in range(1, fi):
        owner = o * fi + lax.rem(i + fi - j, fi)
        arrive(half(owner, c), ag_i, (0, j), inner_dev(j))
        onward(owner)
    for k in (1, 3, 2):
        o_from = lax.rem(o + FO - k, FO)
        owner = o_from * fi + i
        arrive(half(owner, c), ag_o, (k,), outer_dev(k))
        for j in range(1, fi):
            send(half(owner, c), half(owner, c), ag_i, (k, j), inner_dev(j))
        onward(owner)
    for k in (1, 3, 2):
        o_from = lax.rem(o + FO - k, FO)
        for j in range(1, fi):
            owner = o_from * fi + lax.rem(i + fi - j, fi)
            arrive(half(owner, c), ag_i, (k, j), inner_dev(j))
            onward(owner)

    def forward(qq, carry):
        ssq, shv = carry
        span = pl.ds(pl.multiple_of(qq * cq, 128), cq)
        h = res[:, span].astype(F32) + jnp.dot(ctx[...], w[qq], preferred_element_type=F32)
        hid[qq] = h
        v = gain[:, span] * tgt[:, span].astype(F32)
        return (
            ssq + jnp.sum(h * h, axis=1, keepdims=True),
            shv + jnp.sum(h * v, axis=1, keepdims=True),
        )

    zero_t = jnp.zeros((tokens, 1), F32)
    sums = lax.fori_loop(2 * c, 2 * c + 2, forward, (zero_t, zero_t))
    for owner_k in range(1, fsdp_ways):
        owner = lax.rem(f + owner_k, fsdp_ways)
        arrive(half(owner, 1 - c), ag_c, (owner,), core_dev)
    sums = lax.fori_loop(2 - 2 * c, 4 - 2 * c, forward, sums)
    ssq, shv = sums
    rinv = lax.rsqrt(ssq / dw + 1e-06)
    score = shv * rinv
    ratio = jnp.exp(score - base)
    plain = ratio * token_adv
    clipped = jnp.clip(ratio, 0.8, 1.2) * token_adv
    loss_local = jnp.sum(valid * -jnp.minimum(plain, clipped), axis=0, keepdims=True)
    dscore = -valid * jnp.where(plain <= clipped, plain, 0.0) / count1
    lead = dscore * rinv * (32.0 * all_tokens * math.sqrt(dw))
    inner_scale = rinv * rinv * shv / dw

    def make_gh(qq):
        span = pl.ds(pl.multiple_of(qq * cq, 128), cq)
        v = gain[:, span] * tgt[:, span].astype(F32)
        ghs[qq] = (lead * (v - hid[qq] * inner_scale)).astype(BF16)

    for k in (2, 3, 1):
        there = lax.rem(q + k, Q)
        make_gh(there)
        send(ghs.at[there], ghr.at[q], gx, (k,), group_dev(k))
    make_gh(q)
    ghr[q] = ghs[q]
    ls[o, so, i, q] = jnp.broadcast_to(loss_local, (8, 128))
    for k in range(1, Q):
        mine = ls.at[o, so, i, q]
        send(mine, mine, ls1, (k,), group_dev(k))

    for k in range(1, Q):
        arrive(ctxt.at[lax.rem(q + Q - k, Q)], cx, (k,), group_dev(k))
    for k in range(1, Q):
        arrive(ghr.at[lax.rem(q + Q - k, Q)], gx, (k,), group_dev(k))

    def term(owner):
        total = jnp.dot(ctxt[0, rows_of(owner), :], ghr[0], preferred_element_type=F32)
        for a in range(1, Q):
            total += jnp.dot(ctxt[a, rows_of(owner), :], ghr[a], preferred_element_type=F32)
        return total

    order = (2, 1, 3, 0)
    for k in order:
        for j in range(1, fi):
            owner = lax.rem(o + k, FO) * fi + lax.rem(i + j, fi)
            dws[k, j - 1] = term(owner).astype(BF16)
            send(dws.at[k, j - 1], irecv.at[k, j - 1], rs_i, (k, j), inner_dev(j))

    @pl.loop(0, FO)
    def _(k):
        part[k] = term(lax.rem(o + k, FO) * fi + i)

    for k in range(1, Q):
        arrive(ls.at[o, so, i, lax.rem(q + Q - k, Q)], ls1, (k,), group_dev(k))
    for j in range(1, fi):
        mine = ls.at[o, so, i]
        send(mine, mine, ls2, (j,), inner_dev(j))

    for k in order:
        for j in range(1, fi):
            arrive(irecv.at[k, j - 1], rs_i, (k, j), inner_dev(j))
        total = part[k]
        for j in range(1, fi):
            total = total + irecv[k, j - 1].astype(F32)
        if k == 0:
            part[0] = total
        if k != 0 or so_ways > 1:
            obuf[k] = total.astype(BF16)
        for m in range(so_ways):
            if (m, k) != (0, 0):
                send(obuf.at[k], orecv.at[m, k], rs_o, (m, k), outer_dev(k, m))

    for j in range(1, fi):
        arrive(ls.at[o, so, lax.rem(i + fi - j, fi)], ls2, (j,), inner_dev(j))
    for m, k in outer:
        mine = ls.at[o, so]
        send(mine, mine, ls3, (m, k), outer_dev(k, m))

    @pl.loop(0, aw // 256)
    def _(t):
        span = pl.ds(pl.multiple_of(t * 256, 256), 256)
        total = lax.dot_general(
            ghs[0], w[0, span, :], (((1,), (1,)), ((), ())), preferred_element_type=F32
        )
        for a in range(1, Q):
            total += lax.dot_general(
                ghs[a], w[a, span, :], (((1,), (1,)), ((), ())), preferred_element_type=F32
            )
        gctx[:, span] = total.astype(BF16)

    for m, k in outer:
        arrive(orecv.at[m, k], rs_o, (m, k), outer_dev(k, m))
    total = part[0] if so_ways == 1 else obuf[0].astype(F32)
    for k in range(FO):
        both = None
        for m in range(so_ways):
            if (m, k) != (0, 0):
                one = orecv[m, k].astype(F32)
                both = one if both is None else both + one
        if both is not None:
            total = total + both
    scale = 1.0 / math.sqrt(all_tokens)
    fsend[...] = (total * scale).astype(BF16)
    for k in range(1, Q):
        send(fsend, frecv.at[k], fin, (k,), group_dev(k))
    gw[:, pl.ds(pl.multiple_of(q * cq, 128), cq)] = fsend[...].astype(F32)

    for m, k in outer:
        there = ls.at[lax.rem(o + FO - k, FO), lax.rem(so + so_ways - m, so_ways)]
        arrive(there, ls3, (m, k), outer_dev(k, m))
    loss_out[...] = jnp.sum(ls[...], axis=(0, 1, 2, 3)) / count1

    for k in range(1, Q):
        arrive(frecv.at[k], fin, (k,), group_dev(k))
        q_from = lax.rem(q + Q - k, Q)
        gw[:, pl.ds(pl.multiple_of(q_from * cq, 128), cq)] = frecv[k].astype(F32)
    for copy in sent:
        copy.wait_send()


def body(
    context,
    residual,
    target_rows,
    log_norm,
    norm_gain,
    out_proj,
    old_logprob,
    lengths,
    rewards,
    prompt_ids,
    placement,
):
    nrows, lmax, aw = context.shape
    dw = residual.shape[2]
    fsdp_ways = lax.axis_size("fsdp")
    seq_ways = lax.axis_size("seq")
    fi = fsdp_ways // FO
    so_ways = seq_ways // Q
    tokens = nrows * lmax
    blk = aw // fsdp_ways
    cq = dw // Q

    def spread(column):
        return jnp.broadcast_to(column.astype(F32).reshape(nrows, 1), (nrows, 128))

    packet = jnp.concatenate(
        [
            old_logprob,
            spread(rewards),
            spread(prompt_ids),
            spread(lengths),
            spread(placement),
            jnp.zeros((16 - 5 * nrows, 128), F32),
        ],
        axis=0,
    )
    vmem = pl.BlockSpec(memory_space=pltpu.VMEM)
    dma = pltpu.SemaphoreType.DMA
    gctx, gw, loss = pl.pallas_call(
        functools.partial(kernel, (fsdp_ways, seq_ways, nrows, lmax, dw, aw)),
        out_shape=(
            jax.ShapeDtypeStruct((tokens, aw), BF16),
            jax.ShapeDtypeStruct((blk, dw), F32),
            jax.ShapeDtypeStruct((8, 128), F32),
        ),
        in_specs=[vmem] * 7,
        out_specs=(vmem,) * 3,
        scratch_shapes=[
            pltpu.VMEM((Q, aw, cq), BF16),
            pltpu.VMEM((Q, aw, tokens), BF16),
            pltpu.VMEM((Q, tokens, cq), F32),
            pltpu.VMEM((Q, tokens, cq), BF16),
            pltpu.VMEM((Q, tokens, cq), BF16),
            pltpu.VMEM((FO, fi - 1, blk, cq), BF16),
            pltpu.VMEM((FO, fi - 1, blk, cq), BF16),
            pltpu.VMEM((FO, blk, cq), F32),
            pltpu.VMEM((FO, blk, cq), BF16),
            pltpu.VMEM((so_ways, FO, blk, cq), BF16),
            pltpu.VMEM((blk, cq), BF16),
            pltpu.VMEM((Q, blk, cq), BF16),
            pltpu.VMEM((FO, so_ways, fi, Q, 16, 128), F32),
            pltpu.VMEM((FO, so_ways, fi, Q, 8, 128), F32),
            dma((2, FO)),
            dma((2, FO, fi)),
            dma((2, fsdp_ways)),
            dma((2, Q)),
            dma((2, Q)),
            dma((2, FO, fi)),
            dma((2, so_ways, FO)),
            dma((2, Q)),
            dma((2, Q)),
            dma((2, fi)),
            dma((2, so_ways, FO)),
            dma((2, Q)),
            dma((2, fi)),
            dma((2, so_ways, FO)),
        ],
        compiler_params=pltpu.CompilerParams(
            collective_id=0, has_side_effects=True, vmem_limit_bytes=62 << 20
        ),
        cost_estimate=pl.CostEstimate(
            flops=6 * tokens * aw * dw, bytes_accessed=12 * tokens * dw, transcendentals=tokens
        ),
    )(
        context.reshape(tokens, aw),
        residual.reshape(tokens, dw),
        target_rows.reshape(tokens, dw),
        log_norm,
        norm_gain.reshape(1, dw),
        out_proj,
        packet,
    )
    return (gctx.reshape(nrows, lmax, aw), gw, loss[0, 0])


def solution(mesh):
    return jax.shard_map(
        body,
        mesh=mesh,
        in_specs=(
            P("fsdp", "seq", None),
            P("fsdp", "seq", None),
            P("fsdp", "seq", None),
            P("fsdp", "seq"),
            P(),
            P("fsdp", None),
            P("fsdp", "seq"),
            P("fsdp", "seq"),
            P("fsdp", "seq"),
            P("fsdp", "seq"),
            P("fsdp", "seq"),
        ),
        out_specs=(P("fsdp", "seq", None), P("fsdp", None), P()),
        check_vma=False,
    )
```

time: 560 us -> 246 us (0.44)
  waiting for transfers between devices: 351 us -> 0 us
  Pallas kernels: 0 us -> 231 us
  blocking collectives: 122 us -> 0 us
  matrix products: 26.5 us -> 0 us
  local copies, waits for them, and re-layouts: 29.4 us -> 11.6 us
  between operations: 16.9 us -> 0.64 us
  other arithmetic: 12.6 us -> 1.97 us
    pallas_call x0 -> x1, Pallas kernels: none -> 231 us  [body(): pl.pallas_call(functools.partial(kernel, (fsdp_ways, seq_ways, nrows, lma...]
    unnamed x4 -> x0, waiting for transfers between devices: 216 us -> none
    all_gather x1 -> x0, waiting for transfers between devices: 96.3 us -> none  [body(): whole = lax.all_gather(out_proj, 'fsdp', axis=0, tiled=True)]
    psum x2 -> x0, blocking collectives: 84.1 us -> none  [body(): lax.psum((jnp.sum(local_hot * reward_flat[:, None], axis=0), jnp.sum(loca...]
    psum x1 -> x0, waiting for transfers between devices: 39 us -> none  [body(): lax.psum(piece, 'seq').astype(jnp.float32) * (1.0 / math.sqrt(all_tokens))]
    dot_general x3 -> x0, matrix products: 26.5 us -> none  [the longest x1 10.4 us: body(): jnp.dot(context_flat, whole, preferred_element_type=jnp.float32)]
    unnamed x15 -> x2, local copies, waits for them, and re-layouts: 29.4 us -> 6.31 us
    unnamed x2 -> x0, blocking collectives: 21.6 us -> none
  transfers between devices with their start and end apart: 3 -> 0, of which waited for: 3 -> 0; matrix products, arithmetic and copies ran while one was open for 3% -> 0% of each run, Pallas kernels for 0% -> 0%
where the time goes in v1:
time: 246 us; the launch traced here: 245 us
  Pallas kernels  231 us (94%)
  local copies, waits for them, and re-layouts  11.6 us (5%)
    pallas_call x1, Pallas kernels, body(): pl.pallas_call(functools.partial(kernel, (fsdp_ways, seq_ways, nrows, lma...  231 us
    unnamed x2, local copies, waits for them, and re-layouts  6.31 us

profile of v1, /device:TPU:1, one launch (start us, length us, event | category | flops | bytes accessed | tf_op | source)
XLA Modules:
  0.0 245.5 jit_solution(15206234267166595993)
XLA Ops:
  0.6 0.7 convert_bitcast_fusion.1
  1.3 0.1 broadcast_in_dim.36
  1.4 0.7 convert_bitcast_fusion.2
  2.0 0.1 broadcast_in_dim.34
  2.1 0.7 convert_bitcast_fusion
  2.7 0.1 broadcast_in_dim.38
  2.8 0.7 broadcast_in_dim.32
  3.5 1.9 concatenate.3.packet
  5.4 1.3 reshape.24.gain
  6.7 231.2 %shard_map.130 = (bf16[256,2560]{1,0:T(8,128)(2,1)}, f32[320,2560]{1,0:T(8,128)}, f32[8,128]{1,0:T(8,128)}) custom-call(bf16[256,2560]{1,0:T(8,128)(2,1)} %bitcast.13, bf16[256,2560]{1,0:T(8,128)(2,1)} %bitcast.14, bf16[256,2560]{1,0:T(8,128)(2,1)} %bitcast.15, f32[2,128]{1,0:T(2,128)} %lognorm.1, f32[1,2560]{1,0:T(1,128)} %reshape.24.gain, ...), custom_call_target="tpu_custom_call" | custom-call | flops 10066329600 | bytes 7864320 | tf_op jit(solution)/shard_map/pallas_call | solution.py:422
  238.0 1.2 slice.3
  239.1 2.5 %copy.16 = bf16[2,128,2560]{2,1,0:T(8,128)(2,1)} copy(bf16[2,128,2560]{2,1,0:T(8,128)(2,1)} %bitcast.12) | data formatting | bytes 2621440
  241.6 3.9 %copy.17 = f32[320,2560]{1,0:T(8,128)} copy(f32[320,2560]{1,0:T(8,128)} %get-tuple-element.13) | data formatting | bytes 6553600
  (1 shorter events, 0.0 us)

commit v2 on v1

--- a/solution.py
+++ b/solution.py
@@ -11,6 +11,7 @@
 GS = 16
 FO = 4
 Q = 4
+EXTRA = 256
 MESH = pl.DeviceIdType.MESH
 F32 = jnp.float32
 BF16 = jnp.bfloat16
@@ -44,6 +45,7 @@
     ls,
     ag_o,
     ag_i,
+    ag_y,
     ag_c,
     cx,
     gx,
@@ -63,6 +65,7 @@
     tokens = nrows * lmax
     blk = aw // fsdp_ways
     cq = dw // Q
+    extra = EXTRA
     prompts = nrows * fsdp_ways * seq_ways // GS
     prows = max(8, prompts)
     all_tokens = tokens * fsdp_ways * seq_ways
@@ -83,7 +86,11 @@
     def group_dev(k):
         return (f, so * Q + lax.rem(q + k, Q))
 
-    core_dev = (f, so * Q + q + 1 - 2 * c)
+    q_core = q + 1 - 2 * c
+    q_far = lax.rem(q + 2, Q)
+    q_diag = lax.rem(q_core + 2, Q)
+    core_dev = (f, so * Q + q_core)
+    far_dev = (f, so * Q + q_far)
     outer = [(m, k) for k in range(FO) for m in range(so_ways) if (m, k) != (0, 0)]
     barrier = pltpu.get_barrier_semaphore()
     peers = [outer_dev(k, m) for m, k in outer]
@@ -94,6 +101,7 @@
     pl.semaphore_wait(barrier, len(peers))
 
     sent = []
+    ring = (1, 3, 2)
 
     def send(src, dst, sems, index, dev):
         copy = pltpu.make_async_remote_copy(
@@ -120,8 +128,18 @@
     def rows_of(owner):
         return pl.ds(pl.multiple_of(owner * blk, blk), blk)
 
-    def half(owner, side):
-        return w.at[pl.ds(2 * side, 2), rows_of(owner), :]
+    def piece(owner, quarter, kind):
+        if kind == 0:
+            return w.at[quarter, rows_of(owner), :]
+        if kind == 1:
+            return w.at[quarter, rows_of(owner), pl.ds(0, extra)]
+        return w.at[quarter, rows_of(owner), pl.ds(extra, cq - extra)]
+
+    def mine_at(owner, kind):
+        return piece(owner, q if kind == 0 else q_far, kind)
+
+    def cores_at(owner, kind):
+        return piece(owner, q_core if kind == 0 else q_diag, kind)
 
     pk[o, so, i, q] = packet[...]
     for k in range(1, Q):
@@ -130,18 +148,20 @@
 
     for part_q in range(Q):
         w[part_q, rows_of(f), :] = wown[:, part_q * cq : (part_q + 1) * cq]
-    for k in (2, 1, 3):
-        send(half(f, c), half(f, c), ag_o, (k,), outer_dev(k))
     for j in range(1, fi):
-        send(half(f, c), half(f, c), ag_i, (0, j), inner_dev(j))
+        for kind in (0, 1):
+            send(mine_at(f, kind), mine_at(f, kind), ag_i, (kind, 0, j), inner_dev(j))
+    for k in ring:
+        for kind in (0, 1):
+            send(mine_at(f, kind), mine_at(f, kind), ag_o, (kind, k), outer_dev(k))
 
     @pl.loop(0, aw // 256)
     def _(t):
         span = pl.ds(pl.multiple_of(t * 256, 256), 256)
         ctxt[q, span, :] = ctx[:, span].T
 
-    for k in range(1, Q):
-        send(ctxt.at[q], ctxt.at[q], cx, (k,), group_dev(k))
+    send(ctxt.at[q], ctxt.at[q], cx, (1,), far_dev)
+    send(ctxt.at[q], ctxt.at[q], cx, (2,), core_dev)
 
     for k in range(1, Q):
         there = pk.at[o, so, i, lax.rem(q + Q - k, Q)]
@@ -225,26 +245,31 @@
     valid = jnp.concatenate(valid, axis=0)
     count1 = count[:, 0:1]
 
-    def onward(owner):
-        send(half(owner, c), half(owner, c), ag_c, (owner,), core_dev)
+    def onward(owner, kind):
+        if kind == 0:
+            there = piece(owner, q, 2)
+            send(there, there, ag_y, (owner,), far_dev)
+        send(mine_at(owner, kind), mine_at(owner, kind), ag_c, (kind, owner), core_dev)
 
     for j in range(1, fi):
         owner = o * fi + lax.rem(i + fi - j, fi)
-        arrive(half(owner, c), ag_i, (0, j), inner_dev(j))
-        onward(owner)
-    for k in (1, 3, 2):
-        o_from = lax.rem(o + FO - k, FO)
-        owner = o_from * fi + i
-        arrive(half(owner, c), ag_o, (k,), outer_dev(k))
+        for kind in (0, 1):
+            arrive(mine_at(owner, kind), ag_i, (kind, 0, j), inner_dev(j))
+            onward(owner, kind)
+    for k in ring:
+        owner = lax.rem(o + FO - k, FO) * fi + i
+        for kind in (0, 1):
+            here = mine_at(owner, kind)
+            arrive(here, ag_o, (kind, k), outer_dev(k))
+            for j in range(1, fi):
+                send(here, here, ag_i, (kind, k, j), inner_dev(j))
+            onward(owner, kind)
+    for k in ring:
         for j in range(1, fi):
-            send(half(owner, c), half(owner, c), ag_i, (k, j), inner_dev(j))
-        onward(owner)
-    for k in (1, 3, 2):
-        o_from = lax.rem(o + FO - k, FO)
-        for j in range(1, fi):
-            owner = o_from * fi + lax.rem(i + fi - j, fi)
-            arrive(half(owner, c), ag_i, (k, j), inner_dev(j))
-            onward(owner)
+            owner = lax.rem(o + FO - k, FO) * fi + lax.rem(i + fi - j, fi)
+            for kind in (0, 1):
+                arrive(mine_at(owner, kind), ag_i, (kind, k, j), inner_dev(j))
+                onward(owner, kind)
 
     def forward(qq, carry):
         ssq, shv = carry
@@ -258,11 +283,20 @@
         )
 
     zero_t = jnp.zeros((tokens, 1), F32)
-    sums = lax.fori_loop(2 * c, 2 * c + 2, forward, (zero_t, zero_t))
-    for owner_k in range(1, fsdp_ways):
-        owner = lax.rem(f + owner_k, fsdp_ways)
-        arrive(half(owner, 1 - c), ag_c, (owner,), core_dev)
-    sums = lax.fori_loop(2 - 2 * c, 4 - 2 * c, forward, sums)
+    sums = lax.fori_loop(q, q + 1, forward, (zero_t, zero_t))
+    order = [(0, j) for j in range(1, fi)] + [(k, j) for k in ring for j in range(fi)]
+    owners = [lax.rem(o + FO - k, FO) * fi + lax.rem(i + fi - j, fi) for k, j in order]
+    for owner in owners:
+        there = mine_at(owner, 2)
+        arrive(there, ag_y, (owner,), far_dev)
+        send(there, there, ag_c, (2, owner), core_dev)
+    arrive(ctxt.at[q_far], cx, (1,), far_dev)
+    send(ctxt.at[q_far], ctxt.at[q_far], cx, (3,), core_dev)
+    sums = lax.fori_loop(q_far, q_far + 1, forward, sums)
+    for owner in owners:
+        for kind in (0, 1, 2):
+            arrive(cores_at(owner, kind), ag_c, (kind, owner), core_dev)
+    sums = lax.fori_loop(0, 2, lambda t, both: forward(lax.rem(q_core + 2 * t, Q), both), sums)
     ssq, shv = sums
     rinv = lax.rsqrt(ssq / dw + 1e-06)
     score = shv * rinv
@@ -290,8 +324,8 @@
         mine = ls.at[o, so, i, q]
         send(mine, mine, ls1, (k,), group_dev(k))
 
-    for k in range(1, Q):
-        arrive(ctxt.at[lax.rem(q + Q - k, Q)], cx, (k,), group_dev(k))
+    arrive(ctxt.at[q_core], cx, (2,), core_dev)
+    arrive(ctxt.at[q_diag], cx, (3,), core_dev)
     for k in range(1, Q):
         arrive(ghr.at[lax.rem(q + Q - k, Q)], gx, (k,), group_dev(k))
 
@@ -301,7 +335,7 @@
             total += jnp.dot(ctxt[a, rows_of(owner), :], ghr[a], preferred_element_type=F32)
         return total
 
-    order = (2, 1, 3, 0)
+    order = (1, 3, 2, 0)
     for k in order:
         for j in range(1, fi):
             owner = lax.rem(o + k, FO) * fi + lax.rem(i + j, fi)
@@ -363,8 +397,8 @@
             total = total + both
     scale = 1.0 / math.sqrt(all_tokens)
     fsend[...] = (total * scale).astype(BF16)
-    for k in range(1, Q):
-        send(fsend, frecv.at[k], fin, (k,), group_dev(k))
+    send(fsend, frecv.at[1], fin, (1,), far_dev)
+    send(fsend, frecv.at[2], fin, (2,), core_dev)
     gw[:, pl.ds(pl.multiple_of(q * cq, 128), cq)] = fsend[...].astype(F32)
 
     for m, k in outer:
@@ -372,10 +406,13 @@
         arrive(there, ls3, (m, k), outer_dev(k, m))
     loss_out[...] = jnp.sum(ls[...], axis=(0, 1, 2, 3)) / count1
 
-    for k in range(1, Q):
-        arrive(frecv.at[k], fin, (k,), group_dev(k))
-        q_from = lax.rem(q + Q - k, Q)
-        gw[:, pl.ds(pl.multiple_of(q_from * cq, 128), cq)] = frecv[k].astype(F32)
+    arrive(frecv.at[1], fin, (1,), far_dev)
+    send(frecv.at[1], frecv.at[3], fin, (3,), core_dev)
+    gw[:, pl.ds(pl.multiple_of(q_far * cq, 128), cq)] = frecv[1].astype(F32)
+    arrive(frecv.at[2], fin, (2,), core_dev)
+    gw[:, pl.ds(pl.multiple_of(q_core * cq, 128), cq)] = frecv[2].astype(F32)
+    arrive(frecv.at[3], fin, (3,), core_dev)
+    gw[:, pl.ds(pl.multiple_of(q_diag * cq, 128), cq)] = frecv[3].astype(F32)
     for copy in sent:
         copy.wait_send()
 
@@ -443,9 +480,10 @@
             pltpu.VMEM((Q, blk, cq), BF16),
             pltpu.VMEM((FO, so_ways, fi, Q, 16, 128), F32),
             pltpu.VMEM((FO, so_ways, fi, Q, 8, 128), F32),
-            dma((2, FO)),
-            dma((2, FO, fi)),
+            dma((2, 2, FO)),
+            dma((2, 2, FO, fi)),
             dma((2, fsdp_ways)),
+            dma((2, 3, fsdp_ways)),
             dma((2, Q)),
             dma((2, Q)),
             dma((2, FO, fi)),

time: 246 us -> 208 us (0.85)
  Pallas kernels: 231 us -> 193 us
    pallas_call x1, Pallas kernels: 231 us -> 193 us  [body(): pl.pallas_call(functools.partial(kernel, (fsdp_ways, seq_ways, nrows, lma...]
where the time goes in v2:
time: 208 us
  Pallas kernels  193 us (93%)
  local copies, waits for them, and re-layouts  11.6 us (6%)
    pallas_call x1, Pallas kernels, body(): pl.pallas_call(functools.partial(kernel, (fsdp_ways, seq_ways, nrows, lma...  193 us
    unnamed x2, local copies, waits for them, and re-layouts  6.31 us

profile of v2, /device:TPU:1, one launch (start us, length us, event | category | flops | bytes accessed | tf_op | source)
XLA Modules:
  0.0 207.7 jit_solution(13993069700329427938)
XLA Ops:
  0.6 0.7 convert_bitcast_fusion.1
  1.3 0.1 broadcast_in_dim.36
  1.4 0.7 convert_bitcast_fusion.2
  2.0 0.1 broadcast_in_dim.34
  2.1 0.7 convert_bitcast_fusion
  2.7 0.1 broadcast_in_dim.38
  2.8 0.7 broadcast_in_dim.32
  3.5 1.9 concatenate.3.packet
  5.4 1.3 reshape.24.gain
  6.7 193.4 %shard_map.130 = (bf16[256,2560]{1,0:T(8,128)(2,1)}, f32[320,2560]{1,0:T(8,128)}, f32[8,128]{1,0:T(8,128)}) custom-call(bf16[256,2560]{1,0:T(8,128)(2,1)} %bitcast.13, bf16[256,2560]{1,0:T(8,128)(2,1)} %bitcast.14, bf16[256,2560]{1,0:T(8,128)(2,1)} %bitcast.15, f32[2,128]{1,0:T(2,128)} %lognorm.1, f32[1,2560]{1,0:T(1,128)} %reshape.24.gain, ...), custom_call_target="tpu_custom_call" | custom-call | flops 10066329600 | bytes 7864320 | tf_op jit(solution)/shard_map/pallas_call | solution.py:459
  200.2 1.2 slice.3
  201.4 2.5 %copy.16 = bf16[2,128,2560]{2,1,0:T(8,128)(2,1)} copy(bf16[2,128,2560]{2,1,0:T(8,128)(2,1)} %bitcast.12) | data formatting | bytes 2621440
  203.8 3.9 %copy.17 = f32[320,2560]{1,0:T(8,128)} copy(f32[320,2560]{1,0:T(8,128)} %get-tuple-element.13) | data formatting | bytes 6553600
  (1 shorter events, 0.0 us)

commit v3 on v2

--- a/solution.py
+++ b/solution.py
@@ -23,9 +23,13 @@
     res,
     tgt,
     lognorm,
-    gain,
+    gain1,
     wown,
-    packet,
+    old,
+    rewards,
+    prompt_ids,
+    lengths,
+    placement,
     gctx,
     gw,
     loss_out,
@@ -58,6 +62,7 @@
     ls1,
     ls2,
     ls3,
+    gain,
 ):
     fsdp_ways, seq_ways, nrows, lmax, dw, aw = dims
     fi = fsdp_ways // FO
@@ -141,10 +146,19 @@
     def cores_at(owner, kind):
         return piece(owner, q_core if kind == 0 else q_diag, kind)
 
-    pk[o, so, i, q] = packet[...]
+    at_home = (o, so, i, q)
+    pk[at_home] = jnp.zeros((16, 128), F32)
+    pk[at_home + (pl.ds(0, nrows), slice(None))] = old[...]
+    for n, field in enumerate((rewards, prompt_ids, lengths, placement)):
+        for r in range(nrows):
+            pk[at_home + (pl.ds((n + 1) * nrows + r, 1), slice(None))] = jnp.broadcast_to(
+                field[:, r : r + 1].astype(F32), (1, 128)
+            )
     for k in range(1, Q):
         mine = pk.at[o, so, i, q]
         send(mine, mine, pk1, (k,), group_dev(k))
+
+    gain[...] = gain1[...].reshape(1, dw)
 
     for part_q in range(Q):
         w[part_q, rows_of(f), :] = wown[:, part_q * cq : (part_q + 1) * cq]
@@ -163,18 +177,44 @@
     send(ctxt.at[q], ctxt.at[q], cx, (1,), far_dev)
     send(ctxt.at[q], ctxt.at[q], cx, (2,), core_dev)
 
+    def onward(owner, kind):
+        if kind == 0:
+            there = piece(owner, q, 2)
+            send(there, there, ag_y, (owner,), far_dev)
+        send(mine_at(owner, kind), mine_at(owner, kind), ag_c, (kind, owner), core_dev)
+
+    for j in range(1, fi):
+        owner = o * fi + lax.rem(i + fi - j, fi)
+        for kind in (0, 1):
+            arrive(mine_at(owner, kind), ag_i, (kind, 0, j), inner_dev(j))
+            onward(owner, kind)
     for k in range(1, Q):
         there = pk.at[o, so, i, lax.rem(q + Q - k, Q)]
         arrive(there, pk1, (k,), group_dev(k))
     for j in range(1, fi):
         mine = pk.at[o, so, i]
         send(mine, mine, pk2, (j,), inner_dev(j))
+    for k in ring:
+        owner = lax.rem(o + FO - k, FO) * fi + i
+        for kind in (0, 1):
+            here = mine_at(owner, kind)
+            arrive(here, ag_o, (kind, k), outer_dev(k))
+            for j in range(1, fi):
+                send(here, here, ag_i, (kind, k, j), inner_dev(j))
+            onward(owner, kind)
     for j in range(1, fi):
         there = pk.at[o, so, lax.rem(i + fi - j, fi)]
         arrive(there, pk2, (j,), inner_dev(j))
     for m, k in outer:
         mine = pk.at[o, so]
         send(mine, mine, pk3, (m, k), outer_dev(k, m))
+    for k in ring:
+        for j in range(1, fi):
+            owner = lax.rem(o + FO - k, FO) * fi + lax.rem(i + fi - j, fi)
+            for kind in (0, 1):
+                arrive(mine_at(owner, kind), ag_i, (kind, k, j), inner_dev(j))
+                onward(owner, kind)
+
     for m, k in outer:
         there = pk.at[lax.rem(o + FO - k, FO), lax.rem(so + so_ways - m, so_ways)]
         arrive(there, pk3, (m, k), outer_dev(k, m))
@@ -244,32 +284,6 @@
     token_adv = jnp.concatenate(token_adv, axis=0)
     valid = jnp.concatenate(valid, axis=0)
     count1 = count[:, 0:1]
-
-    def onward(owner, kind):
-        if kind == 0:
-            there = piece(owner, q, 2)
-            send(there, there, ag_y, (owner,), far_dev)
-        send(mine_at(owner, kind), mine_at(owner, kind), ag_c, (kind, owner), core_dev)
-
-    for j in range(1, fi):
-        owner = o * fi + lax.rem(i + fi - j, fi)
-        for kind in (0, 1):
-            arrive(mine_at(owner, kind), ag_i, (kind, 0, j), inner_dev(j))
-            onward(owner, kind)
-    for k in ring:
-        owner = lax.rem(o + FO - k, FO) * fi + i
-        for kind in (0, 1):
-            here = mine_at(owner, kind)
-            arrive(here, ag_o, (kind, k), outer_dev(k))
-            for j in range(1, fi):
-                send(here, here, ag_i, (kind, k, j), inner_dev(j))
-            onward(owner, kind)
-    for k in ring:
-        for j in range(1, fi):
-            owner = lax.rem(o + FO - k, FO) * fi + lax.rem(i + fi - j, fi)
-            for kind in (0, 1):
-                arrive(mine_at(owner, kind), ag_i, (kind, k, j), inner_dev(j))
-                onward(owner, kind)
 
     def forward(qq, carry):
         ssq, shv = carry
@@ -399,20 +413,20 @@
     fsend[...] = (total * scale).astype(BF16)
     send(fsend, frecv.at[1], fin, (1,), far_dev)
     send(fsend, frecv.at[2], fin, (2,), core_dev)
-    gw[:, pl.ds(pl.multiple_of(q * cq, 128), cq)] = fsend[...].astype(F32)
+    gw[:, pl.ds(pl.multiple_of(q * cq, 128), cq)] = fsend[...]
 
     for m, k in outer:
         there = ls.at[lax.rem(o + FO - k, FO), lax.rem(so + so_ways - m, so_ways)]
         arrive(there, ls3, (m, k), outer_dev(k, m))
-    loss_out[...] = jnp.sum(ls[...], axis=(0, 1, 2, 3)) / count1
+    loss_out[...] = jnp.sum(ls[...], axis=(0, 1, 2, 3))[0:1, 0:1] / count1
 
     arrive(frecv.at[1], fin, (1,), far_dev)
     send(frecv.at[1], frecv.at[3], fin, (3,), core_dev)
-    gw[:, pl.ds(pl.multiple_of(q_far * cq, 128), cq)] = frecv[1].astype(F32)
+    gw[:, pl.ds(pl.multiple_of(q_far * cq, 128), cq)] = frecv[1]
     arrive(frecv.at[2], fin, (2,), core_dev)
-    gw[:, pl.ds(pl.multiple_of(q_core * cq, 128), cq)] = frecv[2].astype(F32)
+    gw[:, pl.ds(pl.multiple_of(q_core * cq, 128), cq)] = frecv[2]
     arrive(frecv.at[3], fin, (3,), core_dev)
-    gw[:, pl.ds(pl.multiple_of(q_diag * cq, 128), cq)] = frecv[3].astype(F32)
+    gw[:, pl.ds(pl.multiple_of(q_diag * cq, 128), cq)] = frecv[3]
     for copy in sent:
         copy.wait_send()
 
@@ -440,30 +454,16 @@
     blk = aw // fsdp_ways
     cq = dw // Q
 
-    def spread(column):
-        return jnp.broadcast_to(column.astype(F32).reshape(nrows, 1), (nrows, 128))
-
-    packet = jnp.concatenate(
-        [
-            old_logprob,
-            spread(rewards),
-            spread(prompt_ids),
-            spread(lengths),
-            spread(placement),
-            jnp.zeros((16 - 5 * nrows, 128), F32),
-        ],
-        axis=0,
-    )
     vmem = pl.BlockSpec(memory_space=pltpu.VMEM)
     dma = pltpu.SemaphoreType.DMA
     gctx, gw, loss = pl.pallas_call(
         functools.partial(kernel, (fsdp_ways, seq_ways, nrows, lmax, dw, aw)),
         out_shape=(
             jax.ShapeDtypeStruct((tokens, aw), BF16),
-            jax.ShapeDtypeStruct((blk, dw), F32),
-            jax.ShapeDtypeStruct((8, 128), F32),
+            jax.ShapeDtypeStruct((blk, dw), BF16),
+            jax.ShapeDtypeStruct((1, 1), F32),
         ),
-        in_specs=[vmem] * 7,
+        in_specs=[vmem] * 11,
         out_specs=(vmem,) * 3,
         scratch_shapes=[
             pltpu.VMEM((Q, aw, cq), BF16),
@@ -495,6 +495,7 @@
             dma((2, Q)),
             dma((2, fi)),
             dma((2, so_ways, FO)),
+            pltpu.VMEM((1, dw), F32),
         ],
         compiler_params=pltpu.CompilerParams(
             collective_id=0, has_side_effects=True, vmem_limit_bytes=62 << 20
@@ -507,11 +508,15 @@
         residual.reshape(tokens, dw),
         target_rows.reshape(tokens, dw),
         log_norm,
-        norm_gain.reshape(1, dw),
+        norm_gain,
         out_proj,
-        packet,
+        old_logprob,
+        rewards.reshape(1, nrows),
+        prompt_ids.reshape(1, nrows),
+        lengths.reshape(1, nrows),
+        placement.reshape(1, nrows),
     )
-    return (gctx.reshape(nrows, lmax, aw), gw, loss[0, 0])
+    return (gctx.reshape(nrows, lmax, aw), gw.astype(F32), loss.reshape(()))
 
 
 def solution(mesh):

time: 208 us -> 172 us (0.83)
  Pallas kernels: 193 us -> 165 us
  local copies, waits for them, and re-layouts: 11.6 us -> 1.06 us
    pallas_call x1, Pallas kernels: 193 us -> 165 us  [body(): pl.pallas_call(functools.partial(kernel, (fsdp_ways, seq_ways, nrows, lma...]
    unnamed x2 -> x3, local copies, waits for them, and re-layouts: 6.31 us -> 1.06 us
    convert_element_type x0 -> x1, other arithmetic: none -> 3.64 us  [body(): return (gctx.reshape(nrows, lmax, aw), gw.astype(F32), loss.reshape(()))]
where the time goes in v3:
time: 172 us
  Pallas kernels  165 us (96%)
  other arithmetic  3.64 us (2%)
  between operations  2.33 us (1%)
    pallas_call x1, Pallas kernels, body(): pl.pallas_call(functools.partial(kernel, (fsdp_ways, seq_ways, nrows, lma...  165 us
    convert_element_type x1, other arithmetic, body(): return (gctx.reshape(nrows, lmax, aw), gw.astype(F32), loss.reshape(()))  3.64 us

profile of v3, /device:TPU:1, one launch (start us, length us, event | category | flops | bytes accessed | tf_op | source)
XLA Modules:
  0.0 172.3 jit_solution(15412802005206804334)
XLA Ops:
  0.6 165.2 %shard_map.130 = (bf16[256,2560]{1,0:T(8,128)(2,1)}, bf16[320,2560]{1,0:T(8,128)(2,1)}, f32[1,1]{1,0:T(1,128)}) custom-call(bf16[256,2560]{1,0:T(8,128)(2,1)} %bitcast.10, bf16[256,2560]{1,0:T(8,128)(2,1)} %bitcast.11, bf16[256,2560]{1,0:T(8,128)(2,1)} %bitcast.12, f32[2,128]{1,0:T(2,128)} %lognorm.1, f32[2560]{0:T(1024)} %gain1.1, bf16[320,2560]{1,0:T(8,128)(2,1)} %wown.1, ...), custom_call_target="tpu_custom_call" | custom-call | flops 10066329600 | bytes 7864320 | tf_op jit(solution)/shard_map/pallas_call | solution.py:459
  165.9 0.0 copy-start
  165.9 3.6 %convert_element_type.3 = f32[320,2560]{1,0:T(8,128)} convert(bf16[320,2560]{1,0:T(8,128)(2,1)} %get-tuple-element.7) | non-fusion elementwise | flops 819200 | bytes 4915200 | tf_op jit(solution)/shard_map/convert_element_type | solution.py:519
  169.5 0.0 copy-done
  169.5 1.1 copy.16
Async XLA Ops:
  165.9 3.7 %copy-start = (bf16[256,2560]{1,0:T(8,128)(2,1)S(1)}, bf16[256,2560]{1,0:T(8,128)(2,1)}, u32[]{:S(2)}) copy-start(bf16[256,2560]{1,0:T(8,128)(2,1)} %get-tuple-element.6) | copy-start | bytes 3932164
